TPU v7x, 128 devices: a whole 4x4x4 slice. The times are simulated.
128 devices in a mesh: rep: 8 (over y_hi, x), tr: 8 (over y_lo, z), tc: 2 (over core).
Axes of the slice: x: 4, y: 4 (y_hi: 2, y_lo: 2; y = y_hi * 2 + y_lo), z: 4, core: 2. Of those that a mesh axis runs over, the one named last changes fastest.
Arguments:
- tokens: bfloat16 [512, 16, 8, 1600], P(('rep', 'tr'), None, None, 'tc'), may hold values from -6 to 6
- prefix_kv: bfloat16 [512, 256, 512], P(('rep', 'tr'), None, 'tc')
- ssm_state: float32 [512, 16, 3200], P(('rep', 'tr'), None, 'tc'), may hold values from -6 to 6
- conv_state: float32 [512, 3, 3200], P(('rep', 'tr'), None, 'tc'), may hold values from -6 to 6
- prefix_len: int32 [512], replicated, may hold values from 1 to 256
- group_size: int32 [512], replicated, may hold values from 8 to 16
- serve_replica: int32 [512], replicated, may hold values from 0 to 7, as said below
- in_gain: float32 [1600], P('tc'), may hold values from 0.5 to 1.5
- w_query: bfloat16 [1600, 1024], P(('rep', 'tr'), 'tc'), may hold values from -0.15625 to 0.15625
- w_keyval: bfloat16 [1600, 512], P(('rep', 'tr'), 'tc'), may hold values from -0.15625 to 0.15625
- w_inner: bfloat16 [1600, 2, 3200], P(('rep', 'tr'), None, 'tc'), may hold values from -0.15625 to 0.15625
- conv_weight: float32 [4, 3200], P(None, 'tc'), may hold values from -3 to 3
- conv_bias: float32 [3200], P('tc'), may hold values from -3 to 3
- w_xproj: bfloat16 [3200, 132], P('tc'), may hold values from -0.109375 to 0.109375
- dt_weight: bfloat16 [100, 3200], P(None, 'tc'), may hold values from -0.625 to 0.625
- dt_bias: float32 [3200], P('tc'), may hold values from -4.5 to -1
- decay_log: float32 [16, 3200], P(None, 'tc'), may hold values from -1 to 2.5
- skip_gain: float32 [3200], P('tc'), may hold values from 0.5 to 1.5
- w_attn_out: bfloat16 [1024, 1600], P('tc', ('rep', 'tr'))
- w_ssm_out: bfloat16 [3200, 1600], P('tc', ('rep', 'tr'))
- attn_gain: float32 [1600], replicated, may hold values from 0.5 to 1.5
- ssm_gain: float32 [1600], replicated, may hold values from 0.5 to 1.5
Outputs:
- mixed: bfloat16 [512, 16, 8, 1600], P(('rep', 'tr'), None, None, 'tc')
Inputs may be any that keep to these rules, and one draw needn't show every extreme that they name: `serve_replica`: within each aligned block of 8 groups every replica is named equally often.
All inputs are finite; a program needn't handle non-finite values.
Results may differ from a plain program's by a relative error of at most 0.013.
Values may be sent and summed in bfloat16 or wider, within the bound.
A program may use at most 192 MiB of HBM per device.

v0:
```python
import jax
import jax.numpy as jnp
from jax import lax
from jax.sharding import PartitionSpec as P

D = 1600
HD = 64
QH = 16
KVH = 4
EPSILON = 1e-06


def table_pick(served, table):
    matches = served[:, None] == jnp.arange(table.shape[0], dtype=jnp.int32)[None, :]
    return jnp.sum(jnp.where(matches, table[None, :], 0), axis=1)


def prefix_scores(group_query, key_block, length, score_scale):
    scores = (
        jnp.einsum("rtkjd,pkd->rtkjp", group_query, key_block, preferred_element_type=jnp.float32)
        * score_scale
    )
    positions = jnp.arange(key_block.shape[0], dtype=jnp.int32)
    return jnp.where(positions < length, scores, -jnp.inf)


def local(
    tokens,
    prefix_kv,
    ssm_state,
    conv_state,
    prefix_len,
    group_size,
    serve_replica,
    in_gain,
    w_query,
    w_keyval,
    w_inner,
    conv_weight,
    conv_bias,
    w_xproj,
    dt_weight,
    dt_bias,
    decay_log,
    skip_gain,
    w_attn_out,
    w_ssm_out,
    attn_gain,
    ssm_gain,
):
    rep_count = lax.axis_size("rep")
    my_replica = lax.axis_index("rep")
    row_axis = lax.axis_size("tr")
    my_row = lax.axis_index("tr")
    tensor_count = lax.axis_size("tc")
    tensor_index = lax.axis_index("tc")
    group_count, slot_count, new_count, width_part = tokens.shape
    pair_count = group_count // rep_count
    head_dim = HD
    kv_here = KVH // tensor_count
    per_kv = QH // KVH
    heads_here = QH // tensor_count
    score_scale = head_dim ** (-0.5)
    row_count = group_count * slot_count * new_count
    request_count = group_count * slot_count
    route_plan = serve_replica.reshape(rep_count, row_axis, group_count)
    column = lax.dynamic_index_in_dim(route_plan, my_row, 1, keepdims=False)
    orders = jnp.argsort(column, axis=1, stable=True)
    send_order = lax.dynamic_index_in_dim(orders, my_replica, 0, keepdims=False)
    picked = lax.dynamic_slice_in_dim(orders, my_replica * pair_count, pair_count, 1)
    block_ids = jnp.arange(rep_count, dtype=jnp.int32) * row_axis + my_row
    served = (block_ids[:, None] * group_count + picked).reshape(group_count)
    lengths = table_pick(served, prefix_len)
    live_sizes = table_pick(served, group_size)
    moved_tokens, moved_cache = (
        lax.all_to_all(
            jnp.take(tokens, send_order, axis=0), "rep", split_axis=0, concat_axis=0, tiled=True
        ),
        lax.all_to_all(
            jnp.take(prefix_kv, send_order, axis=0), "rep", split_axis=0, concat_axis=0, tiled=True
        ),
    )
    moved_state, moved_conv = (
        lax.all_to_all(
            jnp.take(ssm_state, send_order, axis=0).astype(jnp.bfloat16),
            "rep",
            split_axis=0,
            concat_axis=0,
            tiled=True,
        ).astype(jnp.float32),
        lax.all_to_all(
            jnp.take(conv_state, send_order, axis=0).astype(jnp.bfloat16),
            "rep",
            split_axis=0,
            concat_axis=0,
            tiled=True,
        ).astype(jnp.float32),
    )
    x_rows = moved_tokens.reshape(row_count, width_part).astype(jnp.float32)
    square_sums = lax.psum(jnp.sum(x_rows * x_rows, axis=1), "tc")
    inv_rms = lax.rsqrt(square_sums / D + EPSILON)
    normed_part = (x_rows * inv_rms[:, None] * in_gain[None, :]).astype(jnp.bfloat16)
    normed = lax.all_gather(normed_part, "tc", axis=1, tiled=True)
    channels = w_inner.shape[2]
    inner_cols = w_inner.reshape(w_inner.shape[0], 2 * channels)
    pieces = (
        lax.all_gather(w_query, ("rep", "tr"), axis=0, tiled=True),
        lax.all_gather(w_keyval, ("rep", "tr"), axis=0, tiled=True),
        lax.all_gather(inner_cols, ("rep", "tr"), axis=0, tiled=True),
    )
    query_run = jnp.dot(normed, pieces[0], preferred_element_type=jnp.float32)
    keyval_run = jnp.dot(normed, pieces[1], preferred_element_type=jnp.float32)
    inner_run = jnp.dot(normed, pieces[2], preferred_element_type=jnp.float32)
    query = query_run.astype(jnp.bfloat16).reshape(
        group_count, slot_count, new_count, kv_here, per_kv, head_dim
    )
    keyval = keyval_run.astype(jnp.bfloat16).reshape(
        group_count, slot_count, new_count, kv_here, 2, head_dim
    )
    cache_len = moved_cache.shape[1]
    cache_heads = moved_cache.reshape(group_count, cache_len, kv_here, 2, head_dim)
    causal = jnp.arange(new_count)[None, :] <= jnp.arange(new_count)[:, None]

    def attend(group_args):
        group_query, group_kv, group_cache, length = group_args
        key_all = group_cache[:, :, 0]
        value_all = group_cache[:, :, 1]
        own_scores = (
            jnp.einsum(
                "rtkjd,rskd->rtkjs",
                group_query,
                group_kv[:, :, :, 0],
                preferred_element_type=jnp.float32,
            )
            * score_scale
        )
        own_scores = jnp.where(causal[None, :, None, None, :], own_scores, -jnp.inf)
        own_max = jnp.max(own_scores, axis=4)
        scores = prefix_scores(group_query, key_all, length, score_scale)
        row_max = jnp.maximum(jnp.max(scores, axis=4), own_max)
        prefix_weights = jnp.exp(scores - row_max[..., None])
        row_totals = jnp.sum(prefix_weights, axis=4)
        weighted = jnp.einsum(
            "rtkjp,pkd->rtkjd",
            prefix_weights.astype(jnp.bfloat16),
            value_all,
            preferred_element_type=jnp.float32,
        )
        own_weights = jnp.exp(own_scores - row_max[..., None])
        row_totals = row_totals + jnp.sum(own_weights, axis=4)
        weighted = weighted + jnp.einsum(
            "rtkjs,rskd->rtkjd",
            own_weights.astype(jnp.bfloat16),
            group_kv[:, :, :, 1],
            preferred_element_type=jnp.float32,
        )
        return (
            (weighted / row_totals[..., None])
            .astype(jnp.bfloat16)
            .reshape(slot_count, new_count, heads_here * head_dim)
        )

    heads = lax.map(attend, (query, keyval, cache_heads, lengths)).reshape(
        row_count, heads_here * head_dim
    )
    inner = inner_run.reshape(group_count, slot_count, new_count, 2, channels)
    conv_in = inner[:, :, :, 0]
    gate = inner[:, :, :, 1].reshape(row_count, channels)
    history = jnp.broadcast_to(
        moved_conv[:, None], (group_count, slot_count, moved_conv.shape[1], channels)
    )
    sequence = jnp.concatenate([history, conv_in], axis=2)
    conv_sum = jnp.broadcast_to(conv_bias, (group_count, slot_count, new_count, channels))
    for tap_index in range(conv_weight.shape[0]):
        conv_sum = (
            conv_sum + conv_weight[tap_index] * sequence[:, :, tap_index : tap_index + new_count]
        )
    conv_out = jax.nn.silu(conv_sum).astype(jnp.bfloat16).reshape(row_count, channels)
    projected = lax.psum(
        jnp.dot(conv_out, w_xproj, preferred_element_type=jnp.float32).astype(jnp.bfloat16), "tc"
    ).astype(jnp.float32)
    rank_width = dt_weight.shape[0]
    state_size = decay_log.shape[0]
    step_in = projected[:, :rank_width].astype(jnp.bfloat16)
    input_mix = projected[:, rank_width : rank_width + state_size]
    output_mix = projected[:, rank_width + state_size :]
    step_size = jax.nn.softplus(
        jnp.dot(step_in, dt_weight, preferred_element_type=jnp.float32) + dt_bias
    )
    decay_rate = -jnp.exp(decay_log)

    def token_major(values):
        return values.reshape(request_count, new_count, values.shape[1]).swapaxes(0, 1)

    start_state = jnp.broadcast_to(
        moved_state[:, None], (group_count, slot_count, state_size, channels)
    ).reshape(request_count, state_size, channels)

    def advance(carried, inputs):
        step_now, value_now, mix_in, mix_out = inputs
        carried = (
            jnp.exp(step_now[:, None, :] * decay_rate[None]) * carried
            + (step_now * value_now)[:, None, :] * mix_in[:, :, None]
        )
        result = jnp.sum(carried * mix_out[:, :, None], axis=1) + skip_gain * value_now
        return (carried, result)

    last_state, outputs = lax.scan(
        advance,
        start_state,
        (
            token_major(step_size),
            token_major(conv_out.astype(jnp.float32)),
            token_major(input_mix),
            token_major(output_mix),
        ),
    )
    ssm_out = outputs.swapaxes(0, 1).reshape(row_count, channels)
    gated = (ssm_out * jax.nn.silu(gate)).astype(jnp.bfloat16)
    pieces = (
        lax.all_gather(w_attn_out, ("rep", "tr"), axis=1, tiled=True),
        lax.all_gather(w_ssm_out, ("rep", "tr"), axis=1, tiled=True),
    )
    attn_part = jnp.dot(heads, pieces[0], preferred_element_type=jnp.float32)
    ssm_part = jnp.dot(gated, pieces[1], preferred_element_type=jnp.float32)
    attn_cols, ssm_cols = (
        lax.psum_scatter(
            attn_part.astype(jnp.bfloat16), "tc", scatter_dimension=1, tiled=True
        ).astype(jnp.float32),
        lax.psum_scatter(
            ssm_part.astype(jnp.bfloat16), "tc", scatter_dimension=1, tiled=True
        ).astype(jnp.float32),
    )
    attn_sq, ssm_sq = lax.psum(
        (jnp.sum(attn_cols * attn_cols, axis=1), jnp.sum(ssm_cols * ssm_cols, axis=1)), "tc"
    )
    attn_share = lax.dynamic_slice_in_dim(attn_gain, tensor_index * width_part, width_part, 0)
    ssm_share = lax.dynamic_slice_in_dim(ssm_gain, tensor_index * width_part, width_part, 0)
    attn_rms = lax.rsqrt(attn_sq / D + EPSILON)[:, None]
    ssm_rms = lax.rsqrt(ssm_sq / D + EPSILON)[:, None]
    branch = 0.5 * (attn_share * attn_cols * attn_rms + ssm_share * ssm_cols * ssm_rms)
    live = jnp.arange(slot_count)[None, :] < live_sizes[:, None]
    live_rows = jnp.broadcast_to(live[:, :, None], (group_count, slot_count, new_count)).reshape(
        row_count, 1
    )
    mixed = jnp.where(live_rows, x_rows + branch, 0.0).astype(jnp.bfloat16)
    return mixed.reshape(group_count, slot_count, new_count, width_part)


def solution(mesh):
    placed = (
        P(("rep", "tr"), None, None, "tc"),
        P(("rep", "tr"), None, "tc"),
        P(("rep", "tr"), None, "tc"),
        P(("rep", "tr"), None, "tc"),
        P(),
        P(),
        P(),
        P("tc"),
        P(("rep", "tr"), "tc"),
        P(("rep", "tr"), "tc"),
        P(("rep", "tr"), None, "tc"),
        P(None, "tc"),
        P("tc"),
        P("tc", None),
        P(None, "tc"),
        P("tc"),
        P(None, "tc"),
        P("tc"),
        P("tc", ("rep", "tr")),
        P("tc", ("rep", "tr")),
        P(),
        P(),
    )
    return jax.shard_map(
        local,
        mesh=mesh,
        in_specs=placed,
        out_specs=P(("rep", "tr"), None, None, "tc"),
        check_vma=False,
    )
```

profile of v0, /device:TPU:1, one launch (start us, length us, event | category | flops | bytes accessed | tf_op | source)
XLA Modules:
  0.0 1650.3 jit_solution(8832406001314647902)
XLA Ops:
  13.5 32.2 %all_to_all.20 = bf16[8,16,8,800]{3,2,1,0:T(8,128)(2,1)S(1)} all-to-all(bf16[8,16,8,800]{3,2,1,0:T(8,128)(2,1)S(1)} %broadcast_select_fusion), channel_id=1, replica_groups=mesh['rep'=8,'tr'=8,'tc'=2] {'rep'}, dimensions={0} | all-to-all | bytes 3276800 | tf_op jit(solution)/shard_map/all_to_all | solution.py:76
  46.3 4.3 psum.28
  53.6 3.8 copy.164
  60.2 4.0 all-to-all-start.1
  64.8 163.2 %all-gather.1 = bf16[64,25,256]{2,1,0:T(8,128)(2,1)S(1)} all-gather(bf16[1,25,256]{2,1,0:T(8,128)(2,1)S(1)} %bitcast.200), channel_id=1, replica_groups=mesh['rep'=8,'tr'=8,'tc'=2] {'rep','tr'}, dimensions={0}, use_global_device_ids=true | all-gather | bytes 832000 | tf_op jit(solution)/shard_map/all_gather | solution.py:108
  234.3 3.7 all-to-all-start.3
  239.3 64.2 %all-gather.13.cloned.1.call-done = bf16[64,25,512]{2,1,0:T(8,128)(2,1)} async-done(((bf16[1,25,512]{2,1,0:T(8,128)(2,1)}), bf16[64,25,512]{2,1,0:T(8,128)(2,1)}) %all-gather.13.cloned.1.call-update) | async-done | bytes 1638416 | tf_op jit(solution)/shard_map/all_gather | solution.py:107
  306.1 327.9 %all-gather.15.cloned.1.call-done = bf16[64,25,512]{2,1,0:T(8,128)(2,1)} async-done(((bf16[1,25,512]{2,1,0:T(8,128)(2,1)}), bf16[64,25,512]{2,1,0:T(8,128)(2,1)}) %all-gather.15.cloned.1.call-update) | async-done | bytes 1638416 | tf_op jit(solution)/shard_map/all_gather | solution.py:221
  634.0 3.7 reshape.226
  637.6 58.4 %all-gather.11.cloned.1.call-done = bf16[1024,1600]{0,1:T(8,128)(2,1)} async-done(((bf16[1024,800]{0,1:T(8,128)(2,1)}), bf16[1024,1600]{0,1:T(8,128)(2,1)}) %all-gather.11.cloned.1.call-update) | async-done | bytes 3276816 | tf_op jit(solution)/shard_map/all_gather | solution.py:103
  696.0 4.0 convolution_convert_fusion.2
  706.8 69.8 %while.24 = (s32[]{:T(128)}, bf16[8,16,8,512]{3,2,1,0:T(8,128)(2,1)}, bf16[8,256,2,2,64]{1,4,3,2,0:T(8,128)(2,1)}, s32[8]{0:T(128)S(1)}, bf16[8,16,8,2,4,64]{5,4...) while((s32[]{:T(128)}, bf16[8,16,8,512]{3,2,1,0:T(8,128)(2,1)}, ...), condition=%wide.region_10.11_spmd.clone, body=%wide.region_5.10_spmd.clone.sunk | while | flops 71293248 | bytes 7227317 | solution.py:163
  776.6 234.6 %all-gather.17.cloned.1.call-done = bf16[64,25,3200]{2,1,0:T(8,128)(2,1)} async-done(((bf16[1,25,3200]{2,1,0:T(8,128)(2,1)}), bf16[64,25,3200]{2,1,0:T(8,128)(2,1)}) %all-gather.17.cloned.1.call-update) | async-done | bytes 10240016 | tf_op jit(solution)/shard_map/all_gather | solution.py:109
  1011.2 11.8 reshape.228
  1023.0 19.0 %fusion.52 = f32[1024,3200]{1,0:T(8,128)} fusion(bf16[1024,1600]{0,1:T(8,128)(2,1)} %all-gather.11.cloned.1.call-done, bf16[1600,3200]{1,0:T(8,128)(2,1)} %reshape.228), kind=kOutput, calls=%fused_computation.124 | convolution fusion | flops 10485760000 | bytes 26624000 | tf_op jit(solution)/shard_map/dot_general | solution.py:113
  1042.0 17.6 %reshape.180 = f32[8,16,8,2,1600]{4,3,2,1,0:T(2,128)} reshape(f32[1024,3200]{1,0:T(8,128)} %fusion.52) | data formatting | bytes 26214400 | tf_op jit(solution)/shard_map/reshape | solution.py:166
  1059.6 16.1 fusion.50
  1082.8 15.4 multiply_convert_fusion
  1102.0 4.8 convolution_convert_fusion.1
  1106.9 247.1 %all-gather.19.cloned.1.call-done = bf16[64,25,1600]{2,1,0:T(8,128)(2,1)} async-done(((bf16[1,25,1600]{2,1,0:T(8,128)(2,1)}), bf16[64,25,1600]{2,1,0:T(8,128)(2,1)}) %all-gather.19.cloned.1.call-update) | async-done | bytes 5120016 | tf_op jit(solution)/shard_map/all_gather | solution.py:222
  1354.0 8.8 reshape.230
  1362.8 5.3 copy.170
  1368.2 6.3 copy.192
  1374.4 46.0 %all-reduce.3.cloned.1.call-done = bf16[1024,132]{0,1:T(8,128)(2,1)} async-done(((bf16[1024,132]{0,1:T(8,128)(2,1)}), bf16[1024,132]{0,1:T(8,128)(2,1)}) %all-reduce.3.cloned.1.call-update) | async-done | bytes 270352 | tf_op jit(solution)/shard_map/psum | solution.py:179
  1420.5 7.6 compare_select_fusion
  1428.0 7.5 copy.169
  1436.8 5.9 broadcast_in_dim.164
  1442.7 155.4 %while.23 = (s32[]{:T(128)}, f32[128,16,1600]{2,1,0:T(8,128)}, f32[8,128,1600]{2,1,0:T(8,128)}, f32[8,128,1600]{2,0,1:T(8,128)}, f32[16,1600]{1,0:T(8,128)S(1)},...) while((s32[]{:T(128)}, f32[128,16,1600]{2,1,0:T(8,128)}, ...), condition=%wide.region_17.18_spmd, body=%wide.region_15.17_spmd.sunk | while | flops 20070400 | bytes 37087612 | solution.py:208
  1442.8 3.5 constant_dynamic-slice_fusion.15
  1447.7 12.3 multiply_reduce_fusion.3
  1462.2 3.5 constant_dynamic-slice_fusion.15
  1467.1 12.3 multiply_reduce_fusion.3
  1481.6 3.5 constant_dynamic-slice_fusion.15
  1486.4 12.3 multiply_reduce_fusion.3
  1501.0 3.5 constant_dynamic-slice_fusion.15
  1505.9 12.3 multiply_reduce_fusion.3
  1520.4 3.5 constant_dynamic-slice_fusion.15
  1525.3 12.3 multiply_reduce_fusion.3
  1539.8 3.5 constant_dynamic-slice_fusion.15
  1544.7 12.3 multiply_reduce_fusion.3
  1564.2 12.3 multiply_reduce_fusion.3
  1578.8 3.5 constant_dynamic-slice_fusion.15
  1583.7 12.3 multiply_reduce_fusion.3
  1598.1 8.8 fusion.34
  1607.0 10.2 convolution_convert_fusion
  1617.7 4.9 copy.178
  1624.6 7.8 reduce-scatter.5.cloned.1.call-done
  1636.7 4.1 fusion.40
  (323 shorter events, 153.4 us)
Async XLA Ops:
  6.5 3.3 copy-start
  6.5 297.0 %all-gather.13.cloned.1.call-start = ((), (), s32[]{:S(2)}) async-start(), calls=%async_computation.10 | async-start | bytes 2129920 | tf_op jit(solution)/shard_map/all_gather | solution.py:107
  7.3 626.7 %all-gather.15.cloned.1.call-start = ((), (), s32[]{:S(2)}) async-start(), calls=%async_computation.11 | async-start | bytes 2129920 | tf_op jit(solution)/shard_map/all_gather | solution.py:221
  8.0 42.6 %copy-start.12 = (f32[800]{0:T(1024)S(1)}, f32[800]{0:T(1024)}, u32[]{:S(2)}) copy-start(f32[800]{0:T(1024)} %param.33) | copy-start | bytes 9604
  8.0 688.0 %all-gather.11.cloned.1.call-start = ((), (), s32[]{:S(2)}) async-start(), calls=%async_computation.6 | async-start | bytes 4915200 | tf_op jit(solution)/shard_map/all_gather | solution.py:103
  46.2 11.2 copy-start.7
  46.2 12.2 copy-start.5
  53.6 11.3 copy-start.10
  57.3 173.7 %copy-start.3 = (f32[8,3,1600]{2,0,1:T(8,128)S(1)}, f32[8,3,1600]{2,0,1:T(8,128)}, u32[]{:S(2)}) copy-start(f32[8,3,1600]{2,0,1:T(8,128)} %param.29) | copy-start | bytes 460804
  57.3 175.2 %copy-start.9 = (f32[4,1600]{1,0:T(4,128)S(1)}, f32[4,1600]{1,0:T(4,128)}, u32[]{:S(2)}) copy-start(f32[4,1600]{1,0:T(4,128)} %param.37) | copy-start | bytes 76804
  57.3 175.3 %copy-start.15 = (s32[512]{0:T(512)S(1)}, s32[512]{0:T(512)}, u32[]{:S(2)}) copy-start(s32[512]{0:T(512)} %param.31) | copy-start | bytes 6148
  57.3 175.3 %copy-start.16 = (s32[512]{0:T(512)S(1)}, s32[512]{0:T(512)}, u32[]{:S(2)}) copy-start(s32[512]{0:T(512)} %param.30) | copy-start | bytes 6148
  57.3 176.0 %copy-start.8 = (f32[16,1600]{1,0:T(8,128)S(1)}, f32[16,1600]{1,0:T(8,128)}, u32[]{:S(2)}) copy-start(f32[16,1600]{1,0:T(8,128)} %param.42) | copy-start | bytes 307204
  57.4 953.8 %all-gather.17.cloned.1.call-start = ((), (), s32[]{:S(2)}) async-start(), calls=%async_computation.12 | async-start | bytes 13312000 | tf_op jit(solution)/shard_map/all_gather | solution.py:109
  60.2 174.1 %all-to-all-start.1 = ((bf16[8,256,256]{2,1,0:T(8,128)(2,1)}), bf16[8,256,256]{2,1,0:T(8,128)(2,1)S(1)}, u32[]{:S(2)}, u32[]{:S(2)}) async-start(bf16[8,256,256]{2,1,0:T(8,128)(2,1)} %broadcast_select_fusion.1), calls=%async_computation.1 | async-start | bytes 2097152 | tf_op jit(solution)/shard_map/all_to_all | solution.py:79
  64.2 1289.9 %all-gather.19.cloned.1.call-start = ((), (), s32[]{:S(2)}) async-start(), calls=%async_computation.13 | async-start | bytes 6922240 | tf_op jit(solution)/shard_map/all_gather | solution.py:222
  234.3 844.7 %all-to-all-start.3 = ((bf16[8,3,1600]{2,1,0:T(4,128)(2,1)}), bf16[8,3,1600]{2,1,0:T(4,128)(2,1)S(1)}, u32[]{:S(2)}, u32[]{:S(2)}) async-start(bf16[8,3,1600]{2,1,0:T(4,128)(2,1)} %copy.168), calls=%async_computation.4 | async-start | bytes 212992 | tf_op jit(solution)/shard_map/all_to_all | solution.py:91
  1075.7 7.1 copy-start.11
  1079.0 357.8 %all-to-all-start.2 = ((bf16[8,16,1600]{2,1,0:T(8,128)(2,1)}), bf16[8,16,1600]{2,1,0:T(8,128)(2,1)S(1)}, u32[]{:S(2)}, u32[]{:S(2)}) async-start(bf16[8,16,1600]{2,1,0:T(8,128)(2,1)} %select_convert_fusion), calls=%async_computation.3 | async-start | bytes 851968 | tf_op jit(solution)/shard_map/all_to_all | solution.py:84
  1082.5 338.0 %all-reduce.3.cloned.1.call-start = ((), (), s32[]{:S(2)}) async-start(), calls=%async_computation.8 | async-start | bytes 557056 | tf_op jit(solution)/shard_map/psum | solution.py:179
  1082.8 17.1 %copy-start.18 = (bf16[1600,132]{0,1:T(8,128)(2,1)S(1)}, bf16[1600,132]{0,1:T(8,128)(2,1)}, u32[]{:S(2)}) copy-start(bf16[1600,132]{0,1:T(8,128)(2,1)} %param.39) | copy-start | bytes 1267204
  1082.8 19.2 %copy-start.4 = (bf16[1600,512]{1,0:T(8,128)(2,1)S(1)}, bf16[1600,512]{1,0:T(8,128)(2,1)}, u32[]{:S(2)}) copy-start(bf16[1600,512]{1,0:T(8,128)(2,1)} %reshape.226) | copy-start | bytes 4915204
  1098.2 1.7 copy-start.2
  1102.0 520.7 %reduce-scatter.3.cloned.1.call-start = ((), (), s32[]{:S(2)}) async-start(), calls=%async_computation.7 | async-start | bytes 4915200 | tf_op jit(solution)/shard_map/reduce_scatter | solution.py:227
  1106.9 525.5 %reduce-scatter.5.cloned.1.call-start = ((), (), s32[]{:S(2)}) async-start(), calls=%async_computation.9 | async-start | bytes 4915200 | tf_op jit(solution)/shard_map/reduce_scatter | solution.py:230
  1368.1 52.3 %copy-start.19 = (bf16[100,1600]{1,0:T(8,128)(2,1)S(1)}, bf16[100,1600]{1,0:T(8,128)(2,1)}, u32[]{:S(2)}) copy-start(bf16[100,1600]{1,0:T(8,128)(2,1)} %param.40) | copy-start | bytes 960004
  1368.2 52.3 %copy-start.20 = (f32[1600]{0:T(1024)S(1)}, f32[1600]{0:T(1024)}, u32[]{:S(2)}) copy-start(f32[1600]{0:T(1024)} %param.41) | copy-start | bytes 19204
  1436.8 5.9 copy-start.6
  1607.0 10.3 copy-start.13
  1607.0 10.4 copy-start.14
  1607.0 10.4 copy-start.17
  1622.6 20.6 %copy-start.1 = (bf16[8,16,8,800]{3,2,1,0:T(8,128)(2,1)S(1)}, bf16[8,16,8,800]{3,2,1,0:T(8,128)(2,1)}, u32[]{:S(2)}) copy-start(bf16[8,16,8,800]{3,2,1,0:T(8,128)(2,1)} %param.26) | copy-start | bytes 4915204
Sparse Core Ops, SparseCore 0:
  9.0 294.4 all-gather.12
  305.2 328.7 all-gather.14
  635.6 60.3 all-gather.10
  697.5 313.6 all-gather.16
  1012.7 341.3 all-gather.18
  1356.3 64.0 all-reduce.2
  1422.9 14.9 reduce-scatter.2
  1617.4 14.9 reduce-scatter.4
where the time goes:
time: 1660 us; the launch traced here: 1650 us
  waiting for transfers between devices  988 us (60%)
  blocking collectives  202 us (12%)
  local copies, waits for them, and re-layouts  186 us (11%)
  other arithmetic  177 us (11%)
  matrix products  71.2 us (4%)
    all_gather x1, waiting for transfers between devices, local(): lax.all_gather(w_attn_out, ('rep', 'tr'), axis=1, tiled=True)  328 us
    all_gather x1, waiting for transfers between devices, local(): lax.all_gather(w_ssm_out, ('rep', 'tr'), axis=1, tiled=True)  247 us
    all_gather x1, waiting for transfers between devices, local(): lax.all_gather(inner_cols, ('rep', 'tr'), axis=0, tiled=True)  235 us
    all_gather x1, blocking collectives, local(): lax.all_gather(w_keyval, ('rep', 'tr'), axis=0, tiled=True)  163 us
    reduce_sum x8, other arithmetic, advance(): jnp.sum(carried * mix_out[:, :, None], axis=1) + skip_gain * value_now  98.4 us
    all_gather x1, waiting for transfers between devices, local(): lax.all_gather(w_query, ('rep', 'tr'), axis=0, tiled=True)  64.2 us
    all_gather x1, waiting for transfers between devices, local(): normed = lax.all_gather(normed_part, 'tc', axis=1, tiled=True)  58.4 us
    psum x1, waiting for transfers between devices, local(): lax.psum(jnp.dot(conv_out, w_xproj, preferred_element_type=jnp.float32).a...  46 us
  transfers between devices with their start and end apart: 11, of which 7 were waited for; matrix products, arithmetic and copies ran while one was open for 26% of the time, Pallas kernels for 0%

commit v1 on v0

--- a/solution.py
+++ b/solution.py
@@ -1,3 +1,4 @@
+import functools
 import jax
 import jax.numpy as jnp
 from jax import lax
@@ -8,6 +9,13 @@
 QH = 16
 KVH = 4
 EPSILON = 1e-06
+
+
+def _return_all_bands(body, device_axis):
+    return jnp.sum(lax.all_gather(body, device_axis), axis=0)
+
+
+refer_spans_all = functools.partial(_return_all_bands, device_axis="tc")
 
 
 def table_pick(served, table):
@@ -176,8 +184,8 @@
             conv_sum + conv_weight[tap_index] * sequence[:, :, tap_index : tap_index + new_count]
         )
     conv_out = jax.nn.silu(conv_sum).astype(jnp.bfloat16).reshape(row_count, channels)
-    projected = lax.psum(
-        jnp.dot(conv_out, w_xproj, preferred_element_type=jnp.float32).astype(jnp.bfloat16), "tc"
+    projected = refer_spans_all(
+        jnp.dot(conv_out, w_xproj, preferred_element_type=jnp.float32).astype(jnp.bfloat16)
     ).astype(jnp.float32)
     rank_width = dt_weight.shape[0]
     state_size = decay_log.shape[0]

time: 1660 us -> 1730 us (1.042)
  blocking collectives: 202 us -> 246 us
  waiting for transfers between devices: 988 us -> 1020 us
    all_gather x1, waiting for transfers between devices: 235 us -> 347 us  [local(): lax.all_gather(inner_cols, ('rep', 'tr'), axis=0, tiled=True)]
    psum x1 -> x0, waiting for transfers between devices: 46 us -> none  [local(): lax.psum(jnp.dot(conv_out, w_xproj, preferred_element_type=jnp.float32).a...]
    all_gather x0 -> x1, blocking collectives: none -> 44.3 us  [_return_all_bands(): return jnp.sum(lax.all_gather(body, device_axis), axis=0)]
    all_gather x1, waiting for transfers between devices: 247 us -> 215 us  [local(): lax.all_gather(w_ssm_out, ('rep', 'tr'), axis=1, tiled=True)]
    unnamed x50 -> x56, local copies, waits for them, and re-layouts: 40.4 us -> 38.9 us
  transfers between devices with their start and end apart: 11 -> 10, of which waited for: 7 -> 6; matrix products, arithmetic and copies ran while one was open for 26% -> 24% of each run, Pallas kernels for 0% -> 0%
where the time goes in v1:
time: 1730 us; the launch traced here: 1720 us
  waiting for transfers between devices  1020 us (59%)
  blocking collectives  246 us (14%)
  local copies, waits for them, and re-layouts  182 us (11%)
  other arithmetic  178 us (10%)
  matrix products  67.9 us (4%)
    all_gather x1, waiting for transfers between devices, local(): lax.all_gather(inner_cols, ('rep', 'tr'), axis=0, tiled=True)  347 us
    all_gather x1, waiting for transfers between devices, local(): lax.all_gather(w_attn_out, ('rep', 'tr'), axis=1, tiled=True)  326 us
    all_gather x1, waiting for transfers between devices, local(): lax.all_gather(w_ssm_out, ('rep', 'tr'), axis=1, tiled=True)  215 us
    all_gather x1, blocking collectives, local(): lax.all_gather(w_keyval, ('rep', 'tr'), axis=0, tiled=True)  163 us
    reduce_sum x8, other arithmetic, advance(): jnp.sum(carried * mix_out[:, :, None], axis=1) + skip_gain * value_now  98.8 us
    all_gather x1, waiting for transfers between devices, local(): lax.all_gather(w_query, ('rep', 'tr'), axis=0, tiled=True)  65.8 us
    all_gather x1, waiting for transfers between devices, local(): normed = lax.all_gather(normed_part, 'tc', axis=1, tiled=True)  58.4 us
    all_gather x1, blocking collectives, _return_all_bands(): return jnp.sum(lax.all_gather(body, device_axis), axis=0)  44.3 us
  transfers between devices with their start and end apart: 10, of which 6 were waited for; matrix products, arithmetic and copies ran while one was open for 24% of the time, Pallas kernels for 0%

profile of v1, /device:TPU:1, one launch (start us, length us, event | category | flops | bytes accessed | tf_op | source)
XLA Modules:
  0.0 1724.4 jit_solution(13276612273961805889)
XLA Ops:
  13.5 32.2 %all_to_all.20 = bf16[8,16,8,800]{3,2,1,0:T(8,128)(2,1)S(1)} all-to-all(bf16[8,16,8,800]{3,2,1,0:T(8,128)(2,1)S(1)} %broadcast_select_fusion), channel_id=1, replica_groups=mesh['rep'=8,'tr'=8,'tc'=2] {'rep'}, dimensions={0} | all-to-all | bytes 3276800 | tf_op jit(solution)/shard_map/all_to_all | solution.py:84
  46.3 4.3 psum.21
  53.5 3.8 copy.158
  59.7 4.0 all-to-all-start.1
  64.8 162.6 %all-gather.2 = bf16[64,25,256]{2,1,0:T(8,128)(2,1)S(1)} all-gather(bf16[1,25,256]{2,1,0:T(8,128)(2,1)S(1)} %bitcast.204), channel_id=1, replica_groups=mesh['rep'=8,'tr'=8,'tc'=2] {'rep','tr'}, dimensions={0}, use_global_device_ids=true | all-gather | bytes 832000 | tf_op jit(solution)/shard_map/all_gather | solution.py:116
  238.9 65.8 %all-gather.14.cloned.1.call-done = bf16[64,25,512]{2,1,0:T(8,128)(2,1)} async-done(((bf16[1,25,512]{2,1,0:T(8,128)(2,1)}), bf16[64,25,512]{2,1,0:T(8,128)(2,1)}) %all-gather.14.cloned.1.call-update) | async-done | bytes 1638416 | tf_op jit(solution)/shard_map/all_gather | solution.py:115
  307.3 326.2 %all-gather.16.cloned.1.call-done = bf16[64,25,512]{2,1,0:T(8,128)(2,1)} async-done(((bf16[1,25,512]{2,1,0:T(8,128)(2,1)}), bf16[64,25,512]{2,1,0:T(8,128)(2,1)}) %all-gather.16.cloned.1.call-update) | async-done | bytes 1638416 | tf_op jit(solution)/shard_map/all_gather | solution.py:229
  633.5 3.7 reshape.227
  637.2 58.4 %all-gather.12.cloned.1.call-done = bf16[1024,1600]{0,1:T(8,128)(2,1)} async-done(((bf16[1024,800]{0,1:T(8,128)(2,1)}), bf16[1024,1600]{0,1:T(8,128)(2,1)}) %all-gather.12.cloned.1.call-update) | async-done | bytes 3276816 | tf_op jit(solution)/shard_map/all_gather | solution.py:111
  695.5 4.0 convolution_convert_fusion.2
  706.4 69.8 %while.24 = (s32[]{:T(128)}, bf16[8,16,8,512]{3,2,1,0:T(8,128)(2,1)}, bf16[8,256,2,2,64]{1,4,3,2,0:T(8,128)(2,1)}, s32[8]{0:T(128)S(1)}, bf16[8,16,8,2,4,64]{5,4...) while((s32[]{:T(128)}, bf16[8,16,8,512]{3,2,1,0:T(8,128)(2,1)}, ...), condition=%wide.region_10.11_spmd.clone, body=%wide.region_5.10_spmd.clone.sunk | while | flops 71293248 | bytes 7227317 | solution.py:171
  776.2 5.5 convolution_convert_fusion.1
  781.7 215.2 %all-gather.20.cloned.1.call-done = bf16[64,25,1600]{2,1,0:T(8,128)(2,1)} async-done(((bf16[1,25,1600]{2,1,0:T(8,128)(2,1)}), bf16[64,25,1600]{2,1,0:T(8,128)(2,1)}) %all-gather.20.cloned.1.call-update) | async-done | bytes 5120016 | tf_op jit(solution)/shard_map/all_gather | solution.py:230
  996.9 8.6 reshape.231
  1005.5 346.9 %all-gather.18.cloned.1.call-done = bf16[64,25,3200]{2,1,0:T(8,128)(2,1)} async-done(((bf16[1,25,3200]{2,1,0:T(8,128)(2,1)}), bf16[64,25,3200]{2,1,0:T(8,128)(2,1)}) %all-gather.18.cloned.1.call-update) | async-done | bytes 10240016 | tf_op jit(solution)/shard_map/all_gather | solution.py:117
  1352.4 11.9 reshape.229
  1364.3 19.3 %fusion.52 = f32[1024,3200]{1,0:T(8,128)} fusion(bf16[1024,1600]{0,1:T(8,128)(2,1)} %all-gather.12.cloned.1.call-done, bf16[1600,3200]{1,0:T(8,128)(2,1)} %reshape.229), kind=kOutput, calls=%fused_computation.124 | convolution fusion | flops 10485760000 | bytes 26624000 | tf_op jit(solution)/shard_map/dot_general | solution.py:121
  1383.6 17.1 reshape.180
  1400.6 15.9 fusion.50
  1420.0 3.5 all-to-all-start.2
  1423.7 15.3 multiply_convert_fusion
  1442.1 44.3 %all-gather = bf16[2048,132]{0,1:T(8,128)(2,1)S(1)} all-gather(bf16[1024,132]{0,1:T(8,128)(2,1)S(1)} %convolution_convert_fusion.4), channel_id=2, replica_groups=mesh['rep'=8,'tr'=8,'tc'=2] {'tc'}, dimensions={0}, use_global_device_ids=true | all-gather | bytes 811008 | tf_op jit(solution)/shard_map/all_gather | solution.py:15
  1488.2 6.7 compare_select_fusion
  1498.2 7.6 copy.163
  1506.3 6.0 broadcast_in_dim.164
  1512.3 155.8 %while.23 = (s32[]{:T(128)}, f32[128,16,1600]{2,1,0:T(8,128)}, f32[8,128,1600]{2,1,0:T(8,128)}, f32[8,128,1600]{2,0,1:T(8,128)}, f32[16,1600]{1,0:T(8,128)S(1)},...) while((s32[]{:T(128)}, f32[128,16,1600]{2,1,0:T(8,128)}, ...), condition=%wide.region_17.18_spmd, body=%wide.region_15.17_spmd.sunk | while | flops 20070400 | bytes 37087612 | solution.py:216
  1512.4 3.5 constant_dynamic-slice_fusion.15
  1517.2 12.4 multiply_reduce_fusion.3
  1531.8 3.5 constant_dynamic-slice_fusion.15
  1536.7 12.4 multiply_reduce_fusion.3
  1551.3 3.5 constant_dynamic-slice_fusion.15
  1556.1 12.4 multiply_reduce_fusion.3
  1570.8 3.5 constant_dynamic-slice_fusion.15
  1575.6 12.4 multiply_reduce_fusion.3
  1590.2 3.5 constant_dynamic-slice_fusion.15
  1595.1 12.4 multiply_reduce_fusion.3
  1609.7 3.5 constant_dynamic-slice_fusion.15
  1614.5 12.4 multiply_reduce_fusion.3
  1629.2 3.5 constant_dynamic-slice_fusion.15
  1634.1 12.4 multiply_reduce_fusion.3
  1648.8 3.5 constant_dynamic-slice_fusion.15
  1653.6 12.4 multiply_reduce_fusion.3
  1668.1 3.6 copy.186
  1673.0 8.1 fusion.34
  1681.2 7.5 convolution_convert_fusion
  1689.2 4.9 copy.172
  1696.1 10.4 reduce-scatter.5.cloned.1.call-done
  1710.8 4.1 fusion.40
  (330 shorter events, 155.0 us)
Async XLA Ops:
  6.5 3.3 copy-start
  6.5 298.2 %all-gather.14.cloned.1.call-start = ((), (), s32[]{:S(2)}) async-start(), calls=%async_computation.9 | async-start | bytes 2129920 | tf_op jit(solution)/shard_map/all_gather | solution.py:115
  7.3 626.2 %all-gather.16.cloned.1.call-start = ((), (), s32[]{:S(2)}) async-start(), calls=%async_computation.10 | async-start | bytes 2129920 | tf_op jit(solution)/shard_map/all_gather | solution.py:229
  8.0 42.6 %copy-start.13 = (f32[800]{0:T(1024)S(1)}, f32[800]{0:T(1024)}, u32[]{:S(2)}) copy-start(f32[800]{0:T(1024)} %param.33) | copy-start | bytes 9604
  8.0 687.5 %all-gather.12.cloned.1.call-start = ((), (), s32[]{:S(2)}) async-start(), calls=%async_computation.6 | async-start | bytes 4915200 | tf_op jit(solution)/shard_map/all_gather | solution.py:111
  46.2 11.8 copy-start.6
  53.5 10.2 copy-start.8
  53.5 11.3 copy-start.11
  57.3 173.1 %copy-start.5 = (f32[8,3,1600]{2,0,1:T(8,128)S(1)}, f32[8,3,1600]{2,0,1:T(8,128)}, u32[]{:S(2)}) copy-start(f32[8,3,1600]{2,0,1:T(8,128)} %param.29) | copy-start | bytes 460804
  57.4 174.6 %copy-start.10 = (f32[4,1600]{1,0:T(4,128)S(1)}, f32[4,1600]{1,0:T(4,128)}, u32[]{:S(2)}) copy-start(f32[4,1600]{1,0:T(4,128)} %param.37) | copy-start | bytes 76804
  57.4 174.7 %copy-start.16 = (s32[512]{0:T(512)S(1)}, s32[512]{0:T(512)}, u32[]{:S(2)}) copy-start(s32[512]{0:T(512)} %param.31) | copy-start | bytes 6148
  57.4 174.7 %copy-start.17 = (s32[512]{0:T(512)S(1)}, s32[512]{0:T(512)}, u32[]{:S(2)}) copy-start(s32[512]{0:T(512)} %param.30) | copy-start | bytes 6148
  57.4 175.4 %copy-start.9 = (f32[16,1600]{1,0:T(8,128)S(1)}, f32[16,1600]{1,0:T(8,128)}, u32[]{:S(2)}) copy-start(f32[16,1600]{1,0:T(8,128)} %param.42) | copy-start | bytes 307204
  57.4 939.5 %all-gather.20.cloned.1.call-start = ((), (), s32[]{:S(2)}) async-start(), calls=%async_computation.12 | async-start | bytes 6922240 | tf_op jit(solution)/shard_map/all_gather | solution.py:230
  59.7 174.0 %all-to-all-start.1 = ((bf16[8,256,256]{2,1,0:T(8,128)(2,1)}), bf16[8,256,256]{2,1,0:T(8,128)(2,1)S(1)}, u32[]{:S(2)}, u32[]{:S(2)}) async-start(bf16[8,256,256]{2,1,0:T(8,128)(2,1)} %broadcast_select_fusion.1), calls=%async_computation.1 | async-start | bytes 2097152 | tf_op jit(solution)/shard_map/all_to_all | solution.py:87
  63.7 1288.6 %all-gather.18.cloned.1.call-start = ((), (), s32[]{:S(2)}) async-start(), calls=%async_computation.11 | async-start | bytes 13312000 | tf_op jit(solution)/shard_map/all_gather | solution.py:117
  233.7 1186.2 %all-to-all-start.3 = ((bf16[8,3,1600]{2,1,0:T(4,128)(2,1)}), bf16[8,3,1600]{2,1,0:T(4,128)(2,1)S(1)}, u32[]{:S(2)}, u32[]{:S(2)}) async-start(bf16[8,3,1600]{2,1,0:T(4,128)(2,1)} %copy.162), calls=%async_computation.4 | async-start | bytes 212992 | tf_op jit(solution)/shard_map/all_to_all | solution.py:99
  237.1 1457.0 %reduce-scatter.3.cloned.1.call-start = ((), (), s32[]{:S(2)}) async-start(), calls=%async_computation.7 | async-start | bytes 4915200 | tf_op jit(solution)/shard_map/reduce_scatter | solution.py:235
  1416.6 7.2 copy-start.12
  1420.0 86.4 %all-to-all-start.2 = ((bf16[8,16,1600]{2,1,0:T(8,128)(2,1)}), bf16[8,16,1600]{2,1,0:T(8,128)(2,1)S(1)}, u32[]{:S(2)}, u32[]{:S(2)}) async-start(bf16[8,16,1600]{2,1,0:T(8,128)(2,1)} %select_convert_fusion), calls=%async_computation.3 | async-start | bytes 851968 | tf_op jit(solution)/shard_map/all_to_all | solution.py:92
  1423.4 283.0 %reduce-scatter.5.cloned.1.call-start = ((), (), s32[]{:S(2)}) async-start(), calls=%async_computation.8 | async-start | bytes 4915200 | tf_op jit(solution)/shard_map/reduce_scatter | solution.py:238
  1423.7 17.1 copy-start.19
  1439.1 1.7 copy-start.2
  1439.1 49.1 %copy-start.20 = (bf16[100,1600]{1,0:T(8,128)(2,1)S(1)}, bf16[100,1600]{1,0:T(8,128)(2,1)}, u32[]{:S(2)}) copy-start(bf16[100,1600]{1,0:T(8,128)(2,1)} %param.40) | copy-start | bytes 960004
  1439.1 49.1 %copy-start.21 = (f32[1600]{0:T(1024)S(1)}, f32[1600]{0:T(1024)}, u32[]{:S(2)}) copy-start(f32[1600]{0:T(1024)} %param.41) | copy-start | bytes 19204
  1488.2 6.7 copy-start.3
  1506.3 6.0 copy-start.7
  1668.1 4.9 copy-start.4
  1668.1 13.0 slice-start
  1673.0 8.2 slice-start.1
  1681.2 7.6 copy-start.14
  1681.2 7.7 copy-start.15
  1681.2 7.7 copy-start.18
  1694.1 23.2 %copy-start.1 = (bf16[8,16,8,800]{3,2,1,0:T(8,128)(2,1)S(1)}, bf16[8,16,8,800]{3,2,1,0:T(8,128)(2,1)}, u32[]{:S(2)}) copy-start(bf16[8,16,8,800]{3,2,1,0:T(8,128)(2,1)} %param.26) | copy-start | bytes 4915204
Sparse Core Ops, SparseCore 0:
  9.0 295.6 all-gather.13
  306.4 327.0 all-gather.15
  635.1 60.3 all-gather.11
  697.0 299.8 all-gather.19
  998.4 353.9 all-gather.17
  1354.6 55.2 reduce-scatter.2
  1688.9 17.5 reduce-scatter.4
